TPU v7x, 512 devices: a whole 4x4x16 slice. The times are simulated.
512 devices in a mesh: dp: 4 (over x), ctx: 32 (over z, core), tp: 4 (over y).
Axes of the slice: x: 4, y: 4, z: 16, core: 2. Of those that a mesh axis runs over, the one named last changes fastest.
Arguments:
- inputs: bfloat16 [4, 4096, 8192], P('dp', 'ctx', 'tp'), may hold values from -6 to 6
- grad_out: bfloat16 [4, 4096, 8192], P('dp', 'ctx', 'tp'), may hold values from -6 to 6
- input_map: bfloat16 [4, 4096, 128], P('dp', 'ctx'), may hold values from -0.5 to 0.5
- output_map: bfloat16 [4, 4096, 128], P('dp', 'ctx'), may hold values from -0.25 to 0.25
- step_size: float32 [4, 128, 4096], P('dp', 'tp', 'ctx'), may hold values from 0.3 to 1.5
- log_decay: float32 [4, 128, 4096], P('dp', 'tp', 'ctx'), may hold values from -2 to 0
- skip_gain: float32 [128], P('tp'), may hold values from 0.5 to 1.5
Outputs:
- mixed: bfloat16 [4, 4096, 8192], P('dp', 'ctx', 'tp')
- grad_inputs: bfloat16 [4, 4096, 8192], P('dp', 'ctx', 'tp')
- grad_step: float32 [4, 128, 4096], P('dp', 'tp', 'ctx')
- grad_decay: float32 [4, 128, 4096], P('dp', 'tp', 'ctx')
- grad_input_map: float32 [4, 4096, 128], P('dp', ('ctx', 'tp'))
- grad_output_map: float32 [4, 4096, 128], P('dp', ('ctx', 'tp'))
- grad_skip: float32 [128], P('tp')
All inputs are finite; a program needn't handle non-finite values.
Results may differ from a plain program's by a relative error of at most 0.0011.
Values sent between devices are 32-bit elements; how exact they have to be, the bound alone decides.
No kernel may reach another device: no remote copies, remote signals or barrier semaphores. Data moves between devices by JAX's collectives and lax.ppermute only.
A program may use at most 192 MiB of HBM per device.

v0:
```python
import math
import jax
import jax.numpy as jnp
from jax import lax
from jax.sharding import PartitionSpec as P

precise = lax.Precision.HIGHEST


def entering(part, axis, combine, identity, reverse):
    count = lax.axis_size(axis)
    place = lax.axis_index(axis)
    ahead = count - 1 - place if reverse else place
    gathered = jax.tree.map(lambda a: lax.all_gather(a, axis), part)
    state = jax.tree.map(lambda a, e: jnp.zeros_like(a) + jnp.asarray(e, a.dtype), part, identity)

    def one(hop, state):
        source = count - 1 - hop if reverse else hop
        return combine(
            state, jax.tree.map(lambda a: lax.dynamic_index_in_dim(a, source, 0, False), gathered)
        )

    return lax.fori_loop(0, ahead, one, state)


def combine_pair(earlier, later_part):
    return (earlier[0] * later_part[0], later_part[0][..., None, None] * earlier[1] + later_part[1])


def block_forward(values, in_map, out_map, steps, logs):
    cumulative = jnp.cumsum(logs, axis=-1)
    length = cumulative.shape[-1]
    row_ids = lax.broadcasted_iota(jnp.int32, (length, length), 0)
    column_ids = lax.broadcasted_iota(jnp.int32, (length, length), 1)
    causal = row_ids >= column_ids
    spread = cumulative[..., :, None] - cumulative[..., None, :]
    decays = jnp.where(causal, jnp.exp(jnp.where(causal, spread, 0.0)), 0.0)
    affinity = jnp.einsum("btn,bsn->bts", out_map, in_map, precision=precise)
    mixing = decays * affinity[:, None]
    scaled = values * jnp.transpose(steps, (0, 2, 1))[..., None]
    remain = jnp.exp(cumulative[..., -1:] - cumulative)
    weighted = remain[..., None] * in_map[:, None]
    local_state = jnp.einsum("bshp,bhsn->bhpn", scaled, weighted, precision=precise)
    through = jnp.exp(cumulative[..., -1])
    return (cumulative, decays, mixing, scaled, remain, local_state, through)


def block_output(values, out_map, skip_gain, cumulative, mixing, scaled, incoming):
    within = jnp.einsum("bhts,bshp->bthp", mixing, scaled, precision=precise)
    carried = jnp.einsum("bhpn,btn->bthp", incoming, out_map, precision=precise)
    carried = carried * jnp.transpose(jnp.exp(cumulative), (0, 2, 1))[..., None]
    return (within + carried + skip_gain[:, None] * values, carried)


def block_source(cotangent, out_map, cumulative):
    weighted = jnp.exp(cumulative)[..., None] * out_map[:, None]
    return jnp.einsum("bshp,bhsn->bhpn", cotangent, weighted, precision=precise)


def block_backward(
    values,
    cotangent,
    in_map,
    out_map,
    steps,
    skip_gain,
    cumulative,
    decays,
    mixing,
    scaled,
    remain,
    local_state,
    through,
    incoming,
    carried,
    arriving,
):
    remain_col = jnp.transpose(remain, (0, 2, 1))[..., None]
    starts = jnp.transpose(jnp.exp(cumulative), (0, 2, 1))[..., None]
    steps_col = jnp.transpose(steps, (0, 2, 1))[..., None]
    from_later = jnp.einsum("bhpn,btn->bthp", arriving, in_map, precision=precise)
    state_grad = (
        jnp.einsum("bhst,bshp->bthp", mixing, cotangent, precision=precise)
        + remain_col * from_later
    )
    grad_values = steps_col * state_grad + skip_gain[:, None] * cotangent
    grad_steps = jnp.transpose(jnp.sum(values * state_grad, axis=-1), (0, 2, 1))
    products = jnp.einsum("bthp,bshp->bhts", cotangent, scaled, precision=precise)
    summed = jnp.sum(decays * products, axis=1)
    grad_in_map = jnp.einsum("bts,btn->bsn", summed, out_map, precision=precise) + jnp.einsum(
        "bthp,bhpn->btn", scaled * remain_col, arriving, precision=precise
    )
    grad_out_map = jnp.einsum("bts,bsn->btn", summed, in_map, precision=precise) + jnp.einsum(
        "bthp,bhpn->btn", cotangent * starts, incoming, precision=precise
    )
    paired = mixing * products
    change = jnp.sum(paired, axis=-1) - jnp.sum(paired, axis=-2)
    change = change + jnp.transpose(jnp.sum(cotangent * carried, axis=-1), (0, 2, 1))
    change = change - remain * jnp.transpose(jnp.sum(scaled * from_later, axis=-1), (0, 2, 1))
    final_edge = jnp.sum(arriving * local_state, axis=(2, 3)) + through * jnp.sum(
        arriving * incoming, axis=(2, 3)
    )
    length = change.shape[-1]
    ending = lax.broadcasted_iota(jnp.int32, (length,), 0) == length - 1
    change = change + jnp.where(ending, final_edge[..., None], 0.0)
    grad_logs = lax.cumsum(change, axis=2, reverse=True)
    skip_part = jnp.sum(cotangent * values, axis=(0, 1, 3))
    return (grad_values, grad_steps, grad_in_map, grad_out_map, grad_logs, skip_part)


def shards(inputs, grad_out, input_map, output_map, step_size, log_decay, skip_gain):
    sequences, length, features = inputs.shape
    heads = step_size.shape[1]
    per_head = features // heads
    values = inputs.reshape(sequences, length, heads, per_head).astype(jnp.float32)
    cotangent = grad_out.reshape(sequences, length, heads, per_head).astype(jnp.float32)
    in_map = input_map.astype(jnp.float32)
    out_map = output_map.astype(jnp.float32)
    cumulative, decays, mixing, scaled, remain, local_state, through = block_forward(
        values, in_map, out_map, step_size, log_decay
    )
    source = block_source(cotangent, out_map, cumulative)
    neutral = (jnp.ones_like(through), jnp.zeros_like(local_state))
    ahead = entering((through, local_state), "ctx", combine_pair, neutral, False)
    behind = entering((through, source), "ctx", combine_pair, neutral, True)
    incoming = ahead[1]
    arriving = behind[1]
    mixed, carried = block_output(values, out_map, skip_gain, cumulative, mixing, scaled, incoming)
    results = block_backward(
        values,
        cotangent,
        in_map,
        out_map,
        step_size,
        skip_gain,
        cumulative,
        decays,
        mixing,
        scaled,
        remain,
        local_state,
        through,
        incoming,
        carried,
        arriving,
    )
    grad_values, grad_steps, grad_in_part, grad_out_part, grad_logs, skip_part = results
    grad_in_map, grad_out_map = (
        lax.psum_scatter(grad_in_part, "tp", scatter_dimension=1, tiled=True),
        lax.psum_scatter(grad_out_part, "tp", scatter_dimension=1, tiled=True),
    )
    skip_total = lax.psum(skip_part, ("dp", "ctx"))
    factor = 1.0 / math.sqrt(
        sequences * lax.axis_size("dp") * length * lax.axis_size("ctx") * per_head
    )
    mixed_out = mixed.reshape(sequences, length, features).astype(jnp.bfloat16)
    grad_inputs = grad_values.reshape(sequences, length, features).astype(jnp.bfloat16)
    return (
        mixed_out,
        grad_inputs,
        grad_steps,
        grad_logs,
        grad_in_map,
        grad_out_map,
        skip_total * factor,
    )


def solution(mesh):
    in_specs = (
        P("dp", "ctx", "tp"),
        P("dp", "ctx", "tp"),
        P("dp", "ctx", None),
        P("dp", "ctx", None),
        P("dp", "tp", "ctx"),
        P("dp", "tp", "ctx"),
        P("tp"),
    )
    out_specs = (
        P("dp", "ctx", "tp"),
        P("dp", "ctx", "tp"),
        P("dp", "tp", "ctx"),
        P("dp", "tp", "ctx"),
        P("dp", ("ctx", "tp"), None),
        P("dp", ("ctx", "tp"), None),
        P("tp"),
    )
    return jax.shard_map(shards, mesh=mesh, in_specs=in_specs, out_specs=out_specs, check_vma=False)
```

profile of v0, /device:TPU:2, one launch (start us, length us, event | category | flops | bytes accessed | tf_op | source)
XLA Modules:
  0.0 737.4 jit_solution(14283848565593800011)
XLA Ops:
  9.9 3.2 fusion.3
  13.5 2.4 fusion.16
  16.1 36.1 %all-gather = f32[32,32,1]{1,2,0:T(1,128)S(1)} all-gather(f32[1,32,1]{1,2,0:T(1,128)S(1)} %exp.61), channel_id=2, replica_groups=mesh['dp'=4,'ctx'=32,'tp'=4] {'ctx'}, dimensions={0}, use_global_device_ids=true | all-gather | bytes 4224 | tf_op jit(solution)/shard_map/all_gather | solution.py:14
  52.3 3.1 fusion.20
  55.4 153.7 %all-gather.6.cloned.1.call-done = f32[1024,64,128]{2,1,0:T(8,128)} async-done(((f32[32,64,128]{2,1,0:T(8,128)}), f32[1024,64,128]{2,1,0:T(8,128)}) %all-gather.6.cloned.1.call-update) | async-done | bytes 33554448 | tf_op jit(solution)/shard_map/all_gather | solution.py:14
  209.2 191.1 %all-gather.8.cloned.1.call-done = f32[1024,64,128]{2,1,0:T(8,128)} async-done(((f32[32,64,128]{2,1,0:T(8,128)}), f32[1024,64,128]{2,1,0:T(8,128)}) %all-gather.8.cloned.1.call-update) | async-done | bytes 33554448 | tf_op jit(solution)/shard_map/all_gather | solution.py:14
  400.4 46.3 %while.27 = (s32[]{:T(128)}, f32[1,32,64,128]{3,2,1,0:T(8,128)S(1)}, s32[]{:T(128)}, f32[32,1,32]{2,1,0:T(1,128)S(1)}, f32[32,1,32,64,128]{4,3,2,1,0:T(8,128)}, ...) while((s32[]{:T(128)}, f32[1,32,64,128]{3,2,1,0:T(8,128)S(1)}, s32[]{:T(128)}, f32[32,1,32]{2,1,0:T(1,128)S(1)}, ...), condition=%wide.region_4.5_spmd, body=%wide.region_3.4_spmd.sunk | while | flops 524294 | bytes 3146259 | solution.py:23
  400.4 1.4 bitcast_add_fusion.6
  401.9 1.4 bitcast_add_fusion.6
  403.4 1.4 bitcast_add_fusion.6
  404.9 1.4 bitcast_add_fusion.6
  406.4 1.4 bitcast_add_fusion.6
  415.4 1.4 bitcast_add_fusion.6
  434.8 1.4 bitcast_add_fusion.6
  443.8 1.4 bitcast_add_fusion.6
  446.7 1.6 multiply_reduce_fusion.2
  449.4 1.6 multiply_reduce_fusion.3
  452.4 1.9 convolution_bitcast_fusion.2
  455.5 3.8 fusion.31
  459.3 3.2 multiply_reduce_fusion.4
  462.4 1.9 convolution_bitcast_fusion.3
  466.5 208.1 %psum.7 = f32[32]{0:T(128)S(1)} all-reduce(f32[32]{0:T(128)S(1)} %reduce_sum.113), channel_id=1, replica_groups=mesh['dp'=4,'ctx'=32,'tp'=4] {'dp','ctx'}, use_global_device_ids=true, to_apply=%region_18.19 | all-reduce | flops 32 | bytes 256 | tf_op jit(solution)/shard_map/psum | solution.py:152
  675.4 1.8 reduce_window_sum.22
  677.8 53.1 %reduce-scatter.3.cloned.1.call-done = f32[1,32,128]{2,1,0:T(8,128)} async-done(((f32[1,128,128]{2,1,0:T(8,128)}), f32[1,32,128]{2,1,0:T(8,128)}) %reduce-scatter.3.cloned.1.call-update) | async-done | bytes 16400 | tf_op jit(solution)/shard_map/reduce_scatter | solution.py:149
  (117 shorter events, 44.1 us)
Async XLA Ops:
  7.2 2.7 copy-start.8
  7.2 2.8 copy-start.11
  7.2 201.8 %all-gather.6.cloned.1.call-start = ((), (), s32[]{:S(2)}) async-start(), calls=%async_computation.4 | async-start | bytes 34603008 | tf_op jit(solution)/shard_map/all_gather | solution.py:14
  9.8 3.3 copy-start.4
  9.8 3.4 copy-start.10
  9.9 3.6 copy-start.9
  13.1 387.1 %all-gather.8.cloned.1.call-start = ((), (), s32[]{:S(2)}) async-start(), calls=%async_computation.5 | async-start | bytes 34603008 | tf_op jit(solution)/shard_map/all_gather | solution.py:14
  13.5 41.9 %copy-start.1 = (bf16[1,128,2048]{1,2,0:T(8,128)(2,1)}, bf16[1,128,2048]{1,2,0:T(8,128)(2,1)S(1)}, u32[]{:S(2)}) copy-start(bf16[1,128,2048]{1,2,0:T(8,128)(2,1)S(1)} %copy.84) | copy-start | bytes 1572868
  16.0 661.8 %reduce-scatter.5.cloned.1.call-start = ((), (), s32[]{:S(2)}) async-start(), calls=%async_computation.3 | async-start | bytes 81920 | tf_op jit(solution)/shard_map/reduce_scatter | solution.py:150
  446.7 1.6 copy-start
  448.3 1.0 copy-start.2
  449.4 1.7 copy-start.5
  451.1 4.3 copy-start.12
  455.2 275.7 %reduce-scatter.3.cloned.1.call-start = ((), (), s32[]{:S(2)}) async-start(), calls=%async_computation.2 | async-start | bytes 81920 | tf_op jit(solution)/shard_map/reduce_scatter | solution.py:149
  455.4 3.8 copy-start.3
  455.5 3.8 copy-start.7
  459.3 3.2 copy-start.6
Sparse Core Ops, SparseCore 0:
  13.3 195.7 all-gather.5
  211.1 189.0 all-gather.7
  455.3 18.9 reduce-scatter.4
  675.5 55.2 reduce-scatter.2
where the time goes:
time: 739 us; the launch traced here: 737 us
  waiting for transfers between devices  398 us (54%)
  blocking collectives  244 us (33%)
  other arithmetic  50.2 us (7%)
  matrix products  24.4 us (3%)
  between operations  14.1 us (2%)
    all_gather x2, waiting for transfers between devices, entering(): gathered = jax.tree.map(lambda a: lax.all_gather(a, axis), part)  345 us
    psum x1, blocking collectives, shards(): skip_total = lax.psum(skip_part, ('dp', 'ctx'))  208 us
    reduce_scatter x1, waiting for transfers between devices, shards(): lax.psum_scatter(grad_in_part, 'tp', scatter_dimension=1, tiled=True)  53.1 us
    add x31, other arithmetic, combine_pair(): later_part[0][..., None, None] * earlier[1] + later_part[1]  44.9 us
    all_gather x1, blocking collectives, entering(): gathered = jax.tree.map(lambda a: lax.all_gather(a, axis), part)  36.1 us
  transfers between devices with their start and end apart: 4, of which 3 were waited for; matrix products, arithmetic and copies ran while one was open for 3% of the time, Pallas kernels for 0%

commit v1 on v0

--- a/solution.py
+++ b/solution.py
@@ -1,3 +1,4 @@
+import functools
 import math
 import jax
 import jax.numpy as jnp
@@ -5,6 +6,15 @@
 from jax.sharding import PartitionSpec as P
 
 precise = lax.Precision.HIGHEST
+
+
+def search_tiles(chunk, lane_axis, shard_axis):
+    for pp in (lane_axis, shard_axis):
+        chunk = lax.psum(chunk, pp)
+    return chunk
+
+
+_take_area = functools.partial(search_tiles, lane_axis="dp", shard_axis="ctx")
 
 
 def entering(part, axis, combine, identity, reverse):
@@ -149,7 +159,7 @@
         lax.psum_scatter(grad_in_part, "tp", scatter_dimension=1, tiled=True),
         lax.psum_scatter(grad_out_part, "tp", scatter_dimension=1, tiled=True),
     )
-    skip_total = lax.psum(skip_part, ("dp", "ctx"))
+    skip_total = _take_area(skip_part)
     factor = 1.0 / math.sqrt(
         sequences * lax.axis_size("dp") * length * lax.axis_size("ctx") * per_head
     )

time: 739 us -> 549 us (0.74)
  blocking collectives: 244 us -> 90.4 us
  waiting for transfers between devices: 398 us -> 361 us
    psum x1 -> x2, blocking collectives: 208 us -> 54.4 us  [search_tiles(): chunk = lax.psum(chunk, pp)]
    reduce_scatter x1, waiting for transfers between devices: 53.1 us -> 16.5 us  [shards(): lax.psum_scatter(grad_in_part, 'tp', scatter_dimension=1, tiled=True)]
  transfers between devices with their start and end apart: 4 -> 4, of which waited for: 3 -> 3; matrix products, arithmetic and copies ran while one was open for 3% -> 4% of each run, Pallas kernels for 0% -> 0%
where the time goes in v1:
time: 549 us; the launch traced here: 547 us
  waiting for transfers between devices  361 us (66%)
  blocking collectives  90.4 us (16%)
  other arithmetic  50.2 us (9%)
  matrix products  24.4 us (4%)
  between operations  14.1 us (3%)
    all_gather x2, waiting for transfers between devices, entering(): gathered = jax.tree.map(lambda a: lax.all_gather(a, axis), part)  345 us
    psum x2, blocking collectives, search_tiles(): chunk = lax.psum(chunk, pp)  54.4 us
    add x31, other arithmetic, combine_pair(): later_part[0][..., None, None] * earlier[1] + later_part[1]  44.9 us
    all_gather x1, blocking collectives, entering(): gathered = jax.tree.map(lambda a: lax.all_gather(a, axis), part)  36.1 us
    reduce_scatter x1, waiting for transfers between devices, shards(): lax.psum_scatter(grad_in_part, 'tp', scatter_dimension=1, tiled=True)  16.5 us
  transfers between devices with their start and end apart: 4, of which 3 were waited for; matrix products, arithmetic and copies ran while one was open for 4% of the time, Pallas kernels for 0%

profile of v1, /device:TPU:2, one launch (start us, length us, event | category | flops | bytes accessed | tf_op | source)
XLA Modules:
  0.0 547.1 jit_solution(5717141025166187131)
XLA Ops:
  9.9 3.2 fusion.3
  13.5 2.4 fusion.16
  16.1 36.1 %all-gather = f32[32,32,1]{1,2,0:T(1,128)S(1)} all-gather(f32[1,32,1]{1,2,0:T(1,128)S(1)} %exp.61), channel_id=2, replica_groups=mesh['dp'=4,'ctx'=32,'tp'=4] {'ctx'}, dimensions={0}, use_global_device_ids=true | all-gather | bytes 4224 | tf_op jit(solution)/shard_map/all_gather | solution.py:24
  52.3 3.1 fusion.20
  55.4 153.7 %all-gather.6.cloned.1.call-done = f32[1024,64,128]{2,1,0:T(8,128)} async-done(((f32[32,64,128]{2,1,0:T(8,128)}), f32[1024,64,128]{2,1,0:T(8,128)}) %all-gather.6.cloned.1.call-update) | async-done | bytes 33554448 | tf_op jit(solution)/shard_map/all_gather | solution.py:24
  209.2 191.1 %all-gather.8.cloned.1.call-done = f32[1024,64,128]{2,1,0:T(8,128)} async-done(((f32[32,64,128]{2,1,0:T(8,128)}), f32[1024,64,128]{2,1,0:T(8,128)}) %all-gather.8.cloned.1.call-update) | async-done | bytes 33554448 | tf_op jit(solution)/shard_map/all_gather | solution.py:24
  400.4 46.3 %while.27 = (s32[]{:T(128)}, f32[1,32,64,128]{3,2,1,0:T(8,128)S(1)}, s32[]{:T(128)}, f32[32,1,32]{2,1,0:T(1,128)S(1)}, f32[32,1,32,64,128]{4,3,2,1,0:T(8,128)}, ...) while((s32[]{:T(128)}, f32[1,32,64,128]{3,2,1,0:T(8,128)S(1)}, s32[]{:T(128)}, f32[32,1,32]{2,1,0:T(1,128)S(1)}, ...), condition=%wide.region_4.5_spmd, body=%wide.region_3.4_spmd.sunk | while | flops 524294 | bytes 3146259 | solution.py:33
  400.4 1.4 bitcast_add_fusion.6
  401.9 1.4 bitcast_add_fusion.6
  403.4 1.4 bitcast_add_fusion.6
  406.4 1.4 bitcast_add_fusion.6
  415.4 1.4 bitcast_add_fusion.6
  434.8 1.4 bitcast_add_fusion.6
  443.8 1.4 bitcast_add_fusion.6
  446.7 1.6 multiply_reduce_fusion.2
  449.4 1.6 multiply_reduce_fusion.3
  452.4 1.9 convolution_bitcast_fusion.2
  455.5 3.8 fusion.31
  459.3 3.2 multiply_reduce_fusion.4
  462.4 1.9 convolution_bitcast_fusion.3
  466.5 8.6 %psum.14 = f32[32]{0:T(128)S(1)} all-reduce(f32[32]{0:T(128)S(1)} %reduce_sum.113), channel_id=1, replica_groups=mesh['dp'=4,'ctx'=32,'tp'=4] {'dp'}, use_global_device_ids=true, to_apply=%region_18.19 | all-reduce | flops 32 | bytes 256 | tf_op jit(solution)/shard_map/psum | solution.py:13
  475.1 45.8 %psum.15 = f32[32]{0:T(128)S(1)} all-reduce(f32[32]{0:T(128)S(1)} %psum.14), channel_id=1, replica_groups=mesh['dp'=4,'ctx'=32,'tp'=4] {'ctx'}, use_global_device_ids=true, to_apply=%region_19.20 | all-reduce | flops 32 | bytes 256 | tf_op jit(solution)/shard_map/psum | solution.py:13
  521.7 1.8 reduce_window_sum.22
  524.1 16.5 %reduce-scatter.3.cloned.1.call-done = f32[1,32,128]{2,1,0:T(8,128)} async-done(((f32[1,128,128]{2,1,0:T(8,128)}), f32[1,32,128]{2,1,0:T(8,128)}) %reduce-scatter.3.cloned.1.call-update) | async-done | bytes 16400 | tf_op jit(solution)/shard_map/reduce_scatter | solution.py:159
  (118 shorter events, 45.5 us)
Async XLA Ops:
  7.2 2.7 copy-start.8
  7.2 2.8 copy-start.11
  7.2 201.8 %all-gather.6.cloned.1.call-start = ((), (), s32[]{:S(2)}) async-start(), calls=%async_computation.4 | async-start | bytes 34603008 | tf_op jit(solution)/shard_map/all_gather | solution.py:24
  9.8 3.3 copy-start.4
  9.8 3.4 copy-start.10
  9.9 3.6 copy-start.9
  13.1 387.1 %all-gather.8.cloned.1.call-start = ((), (), s32[]{:S(2)}) async-start(), calls=%async_computation.5 | async-start | bytes 34603008 | tf_op jit(solution)/shard_map/all_gather | solution.py:24
  13.5 41.9 %copy-start.1 = (bf16[1,128,2048]{1,2,0:T(8,128)(2,1)}, bf16[1,128,2048]{1,2,0:T(8,128)(2,1)S(1)}, u32[]{:S(2)}) copy-start(bf16[1,128,2048]{1,2,0:T(8,128)(2,1)S(1)} %copy.84) | copy-start | bytes 1572868
  16.0 508.1 %reduce-scatter.5.cloned.1.call-start = ((), (), s32[]{:S(2)}) async-start(), calls=%async_computation.3 | async-start | bytes 81920 | tf_op jit(solution)/shard_map/reduce_scatter | solution.py:160
  446.7 1.6 copy-start
  448.3 1.0 copy-start.2
  449.4 1.7 copy-start.5
  451.1 4.3 copy-start.12
  455.2 85.4 %reduce-scatter.3.cloned.1.call-start = ((), (), s32[]{:S(2)}) async-start(), calls=%async_computation.2 | async-start | bytes 81920 | tf_op jit(solution)/shard_map/reduce_scatter | solution.py:159
  455.4 3.8 copy-start.3
  455.5 3.8 copy-start.7
  459.3 3.2 copy-start.6
Sparse Core Ops, SparseCore 0:
  13.3 195.7 all-gather.5
  211.1 189.0 all-gather.7
  455.3 18.9 reduce-scatter.4
  521.8 18.6 reduce-scatter.2
